TPU v7x, 512 devices: a whole 4x4x16 slice. The times are simulated.
512 devices in a mesh: tm: 16 (over x, z_hi), lib: 32 (over y, z_lo, core).
Axes of the slice: x: 4, y: 4, z: 16 (z_hi: 4, z_lo: 4; z = z_hi * 4 + z_lo), core: 2. Of those that a mesh axis runs over, the one named last changes fastest.
Arguments:
- record: bfloat16 [24, 8192], P(None, 'tm'), may hold values from -6 to 6
- templates: bfloat16 [32, 16, 4, 24, 64, 256], P('lib', 'tm'), may hold values from -6 to 6
- owner: int32 [32, 2], P('lib'), may hold values from 0 to 15
- slot: int32 [32, 2], P('lib'), may hold values from 0 to 3
- mask: int32 [24], replicated, may hold values 0 or 1
Outputs:
- stacks: bfloat16 [32, 2, 64, 8192], P('lib', None, None, 'tm')
- best: float32 [8192], P('tm')
Inputs may be any that keep to these rules, and one draw needn't show every extreme that they name: owner names a tm index. slot names a held block.
All inputs are finite; a program needn't handle non-finite values.
Results may differ from a plain program's by a relative error of at most 0.005.
Values may be sent and summed in bfloat16 or wider, within the bound.
A program may use at most 64 MiB of HBM per device.

v0:
```python
import jax
import jax.numpy as jnp
from jax import lax
from jax.sharding import PartitionSpec as P


def shifted(x, axis, by):
    count = lax.axis_size(axis)
    pairs = [(i, i + by) for i in range(count) if 0 <= i + by < count]
    return lax.ppermute(x, axis, pairs)


def spread(value, axis, source):
    kept = jnp.where(lax.axis_index(axis) == source, value, 0).astype(value.dtype)
    return lax.psum(kept, axis)


def unfold(segment, taps, span_len):
    return jnp.stack([segment[:, k : k + span_len] for k in range(taps)], axis=1)


def on_device(record, templates, owner, slot, mask):
    channels, samples = record.shape
    tap_count = templates.shape[-1]
    block_size = templates.shape[-2]
    rounds = owner.shape[1]
    incoming = shifted(record[:, :tap_count], "tm", -1)
    extended = jnp.concatenate([record, incoming], axis=1)
    mask_f = mask.astype(jnp.float32)
    count = jnp.maximum(jnp.sum(mask_f), 1.0)
    gain = jnp.sqrt(jnp.float32(tap_count)) / jnp.sqrt(count)
    own_blocks = templates[0, 0]
    squares = extended.astype(jnp.float32) ** 2
    running = jnp.concatenate(
        [jnp.zeros((channels, 1), jnp.float32), jnp.cumsum(squares, axis=1)], axis=1
    )
    energy_all = running[:, tap_count : tap_count + samples] - running[:, :samples]
    weight_all = mask_f[:, None] / jnp.sqrt(jnp.maximum(energy_all, jnp.float32(tap_count / 4)))

    def select_block(turn):
        return lax.dynamic_index_in_dim(own_blocks, slot[0, turn], 0, keepdims=False)

    delivered = [spread(select_block(turn), "tm", owner[0, turn]) for turn in range(rounds)]
    kernels = []
    for turn in range(rounds):
        chosen = delivered[turn].astype(jnp.float32)
        norms = jnp.sqrt(jnp.sum(chosen * chosen, axis=-1, keepdims=True) + 1e-06)
        kernels.append((chosen / norms).astype(jnp.bfloat16))
    joined = jnp.concatenate(kernels, axis=1)
    span_len = 512
    window = unfold(extended, tap_count, span_len)
    corr = jnp.einsum("cmk,ckt->cmt", joined, window, preferred_element_type=jnp.float32)
    stack_f = jnp.einsum("cmt,ct->mt", corr, weight_all) * gain
    pieces = [stack_f]
    whole = jnp.concatenate(pieces, axis=1).reshape(rounds, block_size, samples)
    stacks = whole.astype(jnp.bfloat16)[None]
    local_best = jnp.max(whole.reshape(rounds * block_size, samples), axis=0)
    best = lax.pmax(local_best, "lib")
    return (stacks, best)


def solution(mesh):
    placed = (
        P(None, "tm"),
        P("lib", "tm", None, None, None, None),
        P("lib", None),
        P("lib", None),
        P(),
    )
    return jax.shard_map(
        on_device,
        mesh=mesh,
        in_specs=placed,
        out_specs=(P("lib", None, None, "tm"), P("tm")),
        check_vma=False,
    )
```

profile of v0, /device:TPU:1, one launch (start us, length us, event | category | flops | bytes accessed | tf_op | source)
XLA Modules:
  0.0 363.1 jit_solution(1609856817435156273)
XLA Ops:
  7.2 0.7 slice.792
  7.9 1.3 collective-permute-start
  9.2 1.3 fusion.18
  13.1 1.3 fusion.17
  17.0 2.7 select_bitcast_fusion.1
  19.7 0.7 constant_dynamic-update-slice_fusion.1
  20.5 1.3 constant_dynamic-update-slice_fusion.257
  21.8 1.3 convert_reduce_fusion
  24.5 0.7 constant_dynamic-update-slice_fusion.256
  49.0 0.7 constant_dynamic-update-slice_fusion.220
  54.5 0.7 constant_dynamic-update-slice_fusion.212
  57.9 0.7 constant_dynamic-update-slice_fusion.207
  79.8 0.7 constant_dynamic-update-slice_fusion.175
  115.1 0.7 constant_dynamic-update-slice_fusion.123
  153.3 0.7 constant_dynamic-update-slice_fusion.67
  161.5 0.7 constant_dynamic-update-slice_fusion.55
  179.9 0.7 constant_dynamic-update-slice_fusion.28
  195.0 1.7 reduce-window.6
  200.5 61.8 %all-reduce.4.cloned.1.call-done = (bf16[24,64,256]{2,1,0:T(8,128)(2,1)}, bf16[24,64,256]{2,1,0:T(8,128)(2,1)}) async-done(((bf16[24,64,256]{2,1,0:T(8,128)(2,1)}, bf16[24,64,256]{2,1,0:T(8,128)(2,1)}), (bf16[24,64,256]{2,1,0:T(8,128)(2,1)}, bf16[24,64,256]{2,1,0:T(8,128)(2,1)})) %all-reduce.4.cloned.1.call-update) | async-done | bytes 1572880 | tf_op jit(solution)/shard_map/psum | solution.py:15
  262.4 1.9 fusion.4
  264.2 1.4 fusion.5
  265.7 1.4 fusion.7
  267.1 6.7 %multiply_reduce_fusion = f32[512,128]{0,1:T(8,128)S(1)} fusion(f32[512,24]{0,1:T(8,128)S(1)} %fusion.15, bf16[24,256,512]{2,0,1:T(8,128)(2,1)} %constant_dynamic-update-slice_fusion.2, bf16[24,64,256]{2,1,0:T(8,128)(2,1)S(1)} %fusion.7, bf16[24,64,256]{2,1,0:T(8,128)(2,1)S(1)} %fusion.5), kind=kOutput, calls=%fused_computation | convolution fusion | flops 811532288 | bytes 8175616 | tf_op jit(solution)/shard_map/cmk,ckt->cmt/dot_general | solution.py:52
  274.5 81.8 %pmax.7 = f32[512]{0:T(512)} all-reduce(f32[512]{0:T(512)S(1)} %get-tuple-element.6), channel_id=1, replica_groups=mesh['tm'=16,'lib'=32] {'lib'}, use_global_device_ids=true, to_apply=%region_8.9 | all-reduce | flops 512 | bytes 4096 | tf_op jit(solution)/shard_map/pmax | solution.py:58
  (259 shorter events, 169.4 us)
Async XLA Ops:
  7.2 255.2 %all-reduce.4.cloned.1.call-start = ((), (), s32[]{:S(2)}) async-start(), calls=%async_computation | async-start | bytes 3145728 | tf_op jit(solution)/shard_map/psum | solution.py:15
  7.9 16.5 %collective-permute-start = (bf16[24,256]{1,0:T(8,128)(2,1)S(1)}, bf16[24,256]{1,0:T(8,128)(2,1)S(1)}, u32[]{:S(2)}, u32[]{:S(2)}) collective-permute-start(bf16[24,256]{1,0:T(8,128)(2,1)S(1)} %slice.792), channel_id=1, source_target_pairs={{32,0},{64,32},{96,64},{128,96},{160,128},{192,160},{224,192},{256... | collective-permute-start | bytes 36872 | tf_op jit(solution)/shard_map/ppermute | solution.py:10
Sparse Core Ops, SparseCore 0:
  19.9 242.4 all-reduce.3
where the time goes:
time: 364 us; the launch traced here: 363 us
  local copies, waits for them, and re-layouts  179 us (49%)
  blocking collectives  81.8 us (22%)
  waiting for transfers between devices  61.8 us (17%)
  between operations  20.1 us (6%)
  other arithmetic  11.9 us (3%)
  matrix products  6.7 us (2%)
    unnamed x256, local copies, waits for them, and re-layouts  175 us
    pmax x1, blocking collectives, on_device(): best = lax.pmax(local_best, 'lib')  81.8 us
    psum x1, waiting for transfers between devices, spread(): return lax.psum(kept, axis)  61.8 us
  transfers between devices with their start and end apart: 2, of which 1 were waited for; matrix products, arithmetic and copies ran while one was open for 51% of the time, Pallas kernels for 0%

commit v1 on v0

v1 whole, which is shorter than its diff:
```python
import functools

import jax
import jax.numpy as jnp
from jax import lax
from jax.experimental import pallas as pl
from jax.experimental.pallas import tpu as pltpu
from jax.sharding import PartitionSpec as P

MESH = pl.DeviceIdType.MESH
LANES = 128
SHIFTS = 32
PER = 8
PHASES = LANES // SHIFTS
CHUNK = 4


def kernel(
    n_tm, n_lib, rec, tmpl, owner, slot, mask, out, best,
    blk, own, rsx, cand, rsz, recg, g32, s32, left, u32, wt32, nt, wide_t, acc, sbuf, bl_s, bl_r, lb_r,
    t_sem, bz_s, bz_r, bx_s, bx_r, x_s, x_r, z_s, z_r, o_s, o_r, m_s, m_r, l_s, l_r,
):
    slots, channels, block, taps = tmpl.shape
    samples = rec.shape[1]
    me = lax.axis_index("tm")
    lib = lax.axis_index("lib")
    side = 4
    x, z = me // side, lax.rem(me, side)
    chunks = channels // CHUNK
    per_dev = samples // LANES
    rows = n_tm * per_dev

    def at_x(k):
        return {"tm": lax.rem(x + k, side) * side + z}

    def at_z(k):
        return {"tm": x * side + lax.rem(z + k, side)}

    def at_tm(k):
        return {"tm": lax.rem(me + k, n_tm)}

    def at_lib(k):
        return {"lib": lax.rem(lib + k, n_lib)}

    def send(src, dst, s, r, to):
        return pltpu.make_async_remote_copy(
            src_ref=src, dst_ref=dst, send_sem=s, recv_sem=r, device_id=to, device_id_type=MESH
        )

    load = pltpu.make_async_copy(tmpl, blk, t_sem)
    load.start()
    barrier = pltpu.get_barrier_semaphore()
    for k in range(1, n_tm):
        pl.semaphore_signal(barrier, inc=1, device_id=at_tm(k), device_id_type=MESH)
    for k in range(1, n_lib):
        pl.semaphore_signal(barrier, inc=1, device_id=at_lib(k), device_id_type=MESH)

    for ii in range(per_dev):
        recg[me * per_dev + ii] = rec[:, LANES * ii : LANES * (ii + 1)]
    u32[...] = jnp.zeros_like(u32)
    acc[...] = jnp.zeros_like(acc)
    owner_x = [owner[r] // side for r in range(2)]
    owner_z = [lax.rem(owner[r], side) for r in range(2)]
    load.wait()

    def pick(q, _):
        for r in range(2):
            for cc in range(CHUNK):
                for j in range(side):
                    for h in range(2):
                        own[q, j, 2 * r + h, PER * cc : PER * (cc + 1), :] = blk[
                            slot[r], q * CHUNK + cc, (2 * j + h) * PER : (2 * j + h + 1) * PER, :
                        ]
        return 0

    lax.fori_loop(0, chunks, pick, 0)
    pl.semaphore_wait(barrier, n_tm - 1 + n_lib - 1)

    def rec_z(k):
        part = pl.ds(me * per_dev, per_dev)
        return send(recg.at[part], recg.at[part], bz_s.at[k - 1], bz_r.at[k - 1], at_z(k))

    def rec_x(k):
        part = pl.ds(x * side * per_dev, side * per_dev)
        return send(recg.at[part], recg.at[part], bx_s.at[k - 1], bx_r.at[k - 1], at_x(k))

    def tmpl_x(q, k):
        return send(
            own.at[q, lax.rem(x + k, side)], rsx.at[q, k - 1], x_s.at[q, k - 1], x_r.at[q, k - 1], at_x(k)
        )

    def tmpl_z(q, k):
        return send(
            cand.at[q, lax.rem(z + k, side)], rsz.at[q, k - 1], z_s.at[q, k - 1], z_r.at[q, k - 1], at_z(k)
        )

    order = (2, 1, 3)
    early = chunks // 2
    for k in order:
        rec_z(k).start()
    for q in range(early):
        for k in order:
            tmpl_x(q, k).start()
    for k in order:
        rec_z(k).wait_recv()
    for k in order:
        rec_x(k).start()
    for q in range(early, chunks):
        for k in order:
            tmpl_x(q, k).start()

    def pass_on(q):
        for k in order:
            tmpl_x(q, k).wait_recv()
        for i in range(side):
            v = own[q, x, i]
            for k in range(1, side):
                v = jnp.where(owner_x[i // 2] == lax.rem(x + side - k, side), rsx[q, k - 1, i], v)
            cand[q, i] = v
        for k in order:
            tmpl_z(q, k).start()

    lane = lax.broadcasted_iota(jnp.int32, (1, LANES), 1)

    def spread_out(i, _):
        v = recg[i].astype(jnp.float32)
        g32[pl.ds(i * channels, channels), :] = v
        s32[i] = v * v
        return 0

    step = 11
    full = (rows + 2) // step

    def doubled(by, b, _):
        v = s32[pl.ds(b * step, step + 1)]
        r = pltpu.roll(v, LANES - by, axis=2)
        s32[pl.ds(b * step, step)] = v[:step] + jnp.where(lane[None] < LANES - by, r[:step], r[1:])
        return 0

    def weigh(i, _):
        e = s32[i] + s32[i + 1]
        g = 1.0 / jnp.sqrt(jnp.maximum(e, jnp.float32(taps / 4)))
        wt32[pl.ds(i * channels, channels), :] = g
        return 0

    def windows(c, _):
        raw = [g32[pl.ds(c + channels * k, rows, stride=channels), :] for k in range(3)]
        for e in range(PHASES):
            cut = LANES - SHIFTS * e
            v = raw if e == 0 else [pltpu.roll(a, cut, axis=1) for a in raw]
            for p in range(2):
                w = v[p] if e == 0 else jnp.where(lane < cut, v[p], v[p + 1])
                left[c, rows * e : rows * (e + 1), LANES * p : LANES * (p + 1)] = w.astype(jnp.bfloat16)
            left[c, rows * e : rows * (e + 1), 2 * LANES : 3 * LANES] = v[2].astype(jnp.bfloat16)
        return 0

    mine = z // 2
    own_z = jnp.where(mine == 0, owner_z[0], owner_z[1])

    def correlate(q):
        for k in order:
            tmpl_z(q, k).wait_recv()
        v = cand[q, z]
        for k in range(1, side):
            v = jnp.where(own_z == lax.rem(z + side - k, side), rsz[q, k - 1], v)
        wide = v.astype(jnp.float32)
        inv = 1.0 / jnp.sqrt(jnp.sum(wide * wide, axis=1, keepdims=True) + 1e-06)
        u32[:, :taps] = (wide * inv).astype(jnp.bfloat16).astype(jnp.float32)

        def channel(cc, _):
            c = q * CHUNK + cc
            u = u32[pl.ds(pl.multiple_of(cc * PER, PER), PER), :]
            for s in range(SHIFTS):
                w = u if s == 0 else pltpu.roll(u, s, axis=1)
                for p in range(3):
                    wide_t[p, pl.ds(s, PER, stride=SHIFTS), :] = w[:, LANES * p : LANES * (p + 1)]
            right = jnp.concatenate([wide_t[p].astype(jnp.bfloat16) for p in range(3)], axis=1)
            corr = lax.dot_general(
                left[c], right, (((1,), (1,)), ((), ())),
                preferred_element_type=jnp.float32,
            )
            g = wt32[pl.ds(c, rows, stride=channels), :]
            g = jnp.where(mask[c] != 0, g, 0.0)
            turned = [g] + [pltpu.roll(g, SHIFTS * d, axis=1) for d in range(1, PHASES)]
            for e in range(PHASES):
                tile = turned[(PHASES - 1 - e) % PHASES]
                for grp in range(PHASES - 1):
                    tile = jnp.where(lane // SHIFTS == grp, turned[(grp - e) % PHASES], tile)
                both = jnp.concatenate([tile, tile], axis=1)
                part = slice(rows * e, rows * (e + 1))
                acc[part, :] += corr[part, :] * both
            return 0

        lax.fori_loop(0, CHUNK, channel, 0)

    for q in range(early):
        pass_on(q)
    for k in order:
        rec_x(k).wait_recv()
    lax.fori_loop(0, rows, spread_out, 0)
    g32[pl.ds(rows * channels, 8 * channels), :] = jnp.zeros((8 * channels, LANES), jnp.float32)
    s32[pl.ds(rows, 8)] = jnp.zeros((8, channels, LANES), jnp.float32)
    by = 1
    while by < LANES:
        lax.fori_loop(0, full, functools.partial(doubled, by), 0)
        by *= 2
    lax.fori_loop(0, rows, weigh, 0)
    third = channels // (chunks - early)
    for q in range(early, chunks):
        pass_on(q)
        a = (q - early) * third
        lax.fori_loop(a, a + third, windows, 0)
    for q in range(chunks):
        correlate(q)

    count = mask[0]
    for c in range(1, channels):
        count = count + mask[c]
    count_f = jnp.maximum(jnp.full((8, LANES), count, jnp.int32).astype(jnp.float32), 1.0)
    gain = (jnp.sqrt(jnp.float32(taps)) / jnp.sqrt(count_f))[:1]
    top = None
    for m in range(PER):
        h, mm = m // PHASES, m % PHASES
        v = None
        for e in range(PHASES):
            a = acc[rows * e : rows * (e + 1), LANES * h : LANES * (h + 1)]
            by = (SHIFTS * (e - mm)) % LANES
            a = a if by == 0 else pltpu.roll(a, by, axis=1)
            v = a if e == 0 else jnp.where(lane // SHIFTS == e, a, v)
        v = v * gain
        nt[pl.ds(m, rows, stride=PER), :] = v
        top = v if m == 0 else jnp.maximum(top, v)
    for t in range(n_tm):
        bl_s[t] = top[per_dev * t : per_dev * (t + 1), :]
    for t in range(n_tm):
        for ii in range(per_dev):
            a = (per_dev * t + ii) * PER
            sbuf[t, :, LANES * ii : LANES * (ii + 1)] = nt[a : a + PER, :].astype(jnp.bfloat16)

    def peak_tm(k):
        return send(bl_s.at[lax.rem(me + k, n_tm)], bl_r.at[k - 1], m_s.at[k - 1], m_r.at[k - 1], at_tm(k))

    place = out.at[mine, pl.ds(pl.multiple_of((2 * x + lax.rem(z, 2)) * PER, PER), PER), :]

    def stack_tm(k):
        return send(sbuf.at[lax.rem(me + k, n_tm)], place, o_s.at[k - 1], o_r.at[k - 1], at_tm(k))

    for k in range(1, n_tm):
        peak_tm(k).start()
    for k in range(1, n_tm):
        stack_tm(k).start()
    out[mine, pl.ds(pl.multiple_of((2 * x + lax.rem(z, 2)) * PER, PER), PER), :] = sbuf[me]
    peak = bl_s[me]
    for k in range(1, n_tm):
        peak_tm(k).wait_recv()
        peak = jnp.maximum(peak, bl_r[k - 1])
    lb_r[0] = peak

    def peak_lib(k):
        return send(lb_r.at[0], lb_r.at[k], l_s.at[k - 1], l_r.at[k - 1], at_lib(k))

    for k in range(1, n_lib):
        peak_lib(k).start()
    for k in range(1, n_lib):
        peak_lib(k).wait_recv()
        peak = jnp.maximum(peak, lb_r[k])
    best[...] = peak
    for k in range(1, n_tm):
        stack_tm(k).wait_recv()
    for k in order:
        rec_z(k).wait_send()
        rec_x(k).wait_send()
        for q in range(chunks):
            tmpl_x(q, k).wait_send()
            tmpl_z(q, k).wait_send()
    for k in range(1, n_tm):
        peak_tm(k).wait_send()
        stack_tm(k).wait_send()
    for k in range(1, n_lib):
        peak_lib(k).wait_send()


def on_device(record, templates, owner, slot, mask):
    channels, samples = record.shape
    block, taps = templates.shape[-2:]
    rounds = owner.shape[1]
    n_tm, n_lib = lax.axis_size("tm"), lax.axis_size("lib")
    chunks = channels // CHUNK
    per_dev = samples // LANES
    rows = n_tm * per_dev
    vm, bf, f32 = pltpu.VMEM, jnp.bfloat16, jnp.float32
    dma = pltpu.SemaphoreType.DMA
    vmem = pl.BlockSpec(memory_space=pltpu.VMEM)
    smem = pl.BlockSpec(memory_space=pltpu.SMEM)
    piece = (CHUNK * PER, taps)

    stacks, best = pl.pallas_call(
        functools.partial(kernel, n_tm, n_lib),
        out_shape=(
            jax.ShapeDtypeStruct((rounds, block, samples), bf),
            jax.ShapeDtypeStruct((per_dev, LANES), f32),
        ),
        in_specs=[vmem, pl.BlockSpec(memory_space=pl.ANY), smem, smem, smem],
        out_specs=(vmem, vmem),
        scratch_shapes=[
            vm(templates.shape[2:], bf),
            vm((chunks, 4, 4, *piece), bf),
            vm((chunks, 3, 4, *piece), bf),
            vm((chunks, 4, *piece), bf),
            vm((chunks, 3, *piece), bf),
            vm((rows, channels, LANES), bf),
            vm(((rows + 8) * channels, LANES), f32),
            vm((rows + 8, channels, LANES), f32),
            vm((channels, PHASES * rows, 3 * LANES), bf),
            vm((CHUNK * PER, 3 * LANES), f32),
            vm((rows * channels, LANES), f32),
            vm((rows * PER, LANES), f32),
            vm((3, PER * SHIFTS, LANES), f32),
            vm((PHASES * rows, PER * SHIFTS), f32),
            vm((n_tm, PER, samples), bf),
            vm((n_tm, per_dev, LANES), f32),
            vm((n_tm - 1, per_dev, LANES), f32),
            vm((n_lib, per_dev, LANES), f32),
            dma,
            dma((3,)), dma((3,)), dma((3,)), dma((3,)),
            dma((chunks, 3)), dma((chunks, 3)), dma((chunks, 3)), dma((chunks, 3)),
            dma((n_tm - 1,)), dma((n_tm - 1,)), dma((n_tm - 1,)), dma((n_tm - 1,)),
            dma((n_lib - 1,)), dma((n_lib - 1,)),
        ],
        compiler_params=pltpu.CompilerParams(
            collective_id=0, has_side_effects=True, vmem_limit_bytes=48 << 20
        ),
        name="match",
    )(record, templates[0, 0], owner[0], slot[0], mask)
    return stacks[None], best.reshape(samples)


def solution(mesh):
    placed = (
        P(None, "tm"),
        P("lib", "tm", None, None, None, None),
        P("lib", None),
        P("lib", None),
        P(),
    )
    return jax.shard_map(
        on_device,
        mesh=mesh,
        in_specs=placed,
        out_specs=(P("lib", None, None, "tm"), P("tm")),
        check_vma=False,
    )
```

time: 364 us -> 83.6 us (0.23)
  local copies, waits for them, and re-layouts: 179 us -> 5.82 us
  blocking collectives: 81.8 us -> 0 us
  Pallas kernels: 0 us -> 76.9 us
  waiting for transfers between devices: 61.8 us -> 0 us
  between operations: 20.1 us -> 0.65 us
  other arithmetic: 11.9 us -> 0 us
  matrix products: 6.7 us -> 0 us
    unnamed x256 -> x12, local copies, waits for them, and re-layouts: 175 us -> 5.82 us
    pmax x1 -> x0, blocking collectives: 81.8 us -> none  [on_device(): best = lax.pmax(local_best, 'lib')]
    pallas_call x0 -> x1, Pallas kernels: none -> 76.9 us  [on_device(): pl.pallas_call(functools.partial(kernel, n_tm, n_lib), out_shape=(jax.Sha...]
    psum x1 -> x0, waiting for transfers between devices: 61.8 us -> none  [spread(): return lax.psum(kept, axis)]
    dot_general x1 -> x0, matrix products: 6.7 us -> none  [on_device(): jnp.einsum('cmk,ckt->cmt', joined, window, preferred_element_type=jnp.flo...]
  transfers between devices with their start and end apart: 2 -> 0, of which waited for: 1 -> 0; matrix products, arithmetic and copies ran while one was open for 51% -> 0% of each run, Pallas kernels for 0% -> 0%
where the time goes in v1:
time: 83.6 us; the launch traced here: 83.4 us
  Pallas kernels  76.9 us (92%)
  local copies, waits for them, and re-layouts  5.82 us (7%)
    pallas_call x1, Pallas kernels, on_device(): pl.pallas_call(functools.partial(kernel, n_tm, n_lib), out_shape=(jax.Sha...  76.9 us
    unnamed x12, local copies, waits for them, and re-layouts  5.82 us

profile of v1, /device:TPU:1, one launch (start us, length us, event | category | flops | bytes accessed | tf_op | source)
XLA Modules:
  0.0 83.4 jit_solution(15453127595535927578)
XLA Ops:
  0.6 0.0 copy-start
  0.6 1.9 %copy-done = bf16[1,1,4,24,64,256]{5,4,3,2,1,0:T(8,128)(2,1)S(1)} copy-done((bf16[1,1,4,24,64,256]{5,4,3,2,1,0:T(8,128)(2,1)S(1)}, bf16[1,1,4,24,64,256]{5,4,3,2,1,0:T(8,128)(2,1)}, u32[]{:S(2)}) %copy-start) | copy-done | bytes 3145752
  2.5 0.0 copy-start.1
  2.5 0.7 copy-done.1
  3.3 0.0 copy-start.2
  3.3 0.7 copy-done.2
  3.9 0.0 copy-start.3
  3.9 0.7 copy-done.3
  4.6 0.0 copy-start.4
  4.6 0.7 copy-done.4
  5.2 76.9 %match.1 = (bf16[2,64,512]{2,1,0:T(8,128)(2,1)S(1)}, f32[4,128]{1,0:T(4,128)S(1)}) custom-call(bf16[24,512]{1,0:T(8,128)(2,1)S(1)} %copy-done.1, bf16[4,24,64,256]{3,2,1,0:T(8,128)(2,1)S(1)} %bitcast.5, s32[2]{0:T(128)S(1)} %bitcast.8, s32[2]{0:T(128)S(1)} %bitcast.9, s32[24]{0:T(128)S(1)} %copy-done.4), custom_call_target="tpu_custom_call" | custom-call | tf_op jit(solution)/shard_map/match/pallas_call | solution.py:297
  82.1 0.7 copy.9
  82.8 0.6 copy.10
Async XLA Ops:
  0.6 1.9 %copy-start = (bf16[1,1,4,24,64,256]{5,4,3,2,1,0:T(8,128)(2,1)S(1)}, bf16[1,1,4,24,64,256]{5,4,3,2,1,0:T(8,128)(2,1)}, u32[]{:S(2)}) copy-start(bf16[1,1,4,24,64,256]{5,4,3,2,1,0:T(8,128)(2,1)} %param.6) | copy-start | bytes 9437188
  2.5 0.7 copy-start.1
  3.3 0.7 copy-start.2
  3.9 0.7 copy-start.3
  4.6 0.7 copy-start.4

commit v2 on v1

v2 whole, which is shorter than its diff:
```python
import functools

import jax
import jax.numpy as jnp
from jax import lax
from jax.experimental import pallas as pl
from jax.experimental.pallas import tpu as pltpu
from jax.sharding import PartitionSpec as P

MESH = pl.DeviceIdType.MESH
LANES = 128
HALF = LANES // 2
SHIFTS = 32
PER = 8
SIDE = 4
CHUNK = 2


def kernel(
    n_tm, n_lib, rec_h, tmpl, owner_h, slot_h, mask_h, out, best,
    rec, owner, slot, mask, blk, own, rsx, cand, rsz, recg, g32, right, lhs, wt32, tile, nt, acc,
    sbuf, bl_s, bl_r, near_b, far_b,
    in_sem, bz_s, bz_r, bx_s, bx_r, x_s, x_r, z_s, z_r, o_s, o_r, m_s, m_r, n_s, n_r, f_s, f_r,
):
    slots, channels, block, taps = tmpl.shape
    samples = rec.shape[1]
    me = lax.axis_index("tm")
    lib = lax.axis_index("lib")
    x, z = me // SIDE, lax.rem(me, SIDE)
    near = n_lib // SIDE
    far_at, near_at = lib // near, lax.rem(lib, near)
    chunks = channels // CHUNK
    per_dev = samples // LANES
    rows = n_tm * per_dev
    f32, bf = jnp.float32, jnp.bfloat16

    def at_x(k):
        return {"tm": lax.rem(x + k, SIDE) * SIDE + z}

    def at_z(k):
        return {"tm": x * SIDE + lax.rem(z + k, SIDE)}

    def at_tm(k):
        return {"tm": lax.rem(me + k, n_tm)}

    def at_near(k):
        return {"lib": far_at * near + lax.rem(near_at + k, near)}

    def at_far(k):
        return {"lib": lax.rem(far_at + k, SIDE) * near + near_at}

    def send(src, dst, s, r, to):
        return pltpu.make_async_remote_copy(
            src_ref=src, dst_ref=dst, send_sem=s, recv_sem=r, device_id=to, device_id_type=MESH
        )

    loads = [
        pltpu.make_async_copy(a, b, in_sem.at[n])
        for n, (a, b) in enumerate(
            ((slot_h, slot), (tmpl, blk), (rec_h, rec), (owner_h, owner), (mask_h, mask))
        )
    ]
    barrier = pltpu.get_barrier_semaphore()
    peers = [at_z(k) for k in range(1, SIDE)] + [at_x(k) for k in range(1, SIDE)]
    peers += [at_near(k) for k in range(1, near)] + [at_far(k) for k in range(1, SIDE)]
    for to in peers:
        pl.semaphore_signal(barrier, inc=1, device_id=to, device_id_type=MESH)
    for copy in loads:
        copy.start()

    lane = lax.broadcasted_iota(jnp.int32, (1, LANES), 1)
    acc[...] = jnp.zeros_like(acc)
    used = taps + SHIFTS
    right[:, used:, :] = jnp.zeros((channels, right.shape[1] - used, 2 * LANES), bf)
    g32[pl.ds(rows * channels, (LANES - rows) * channels), :] = jnp.zeros(
        ((LANES - rows) * channels, LANES), f32
    )
    for n in (0, 2, 3, 4):
        loads[n].wait()
    for ii in range(per_dev):
        recg[me * per_dev + ii] = rec[:, LANES * ii : LANES * (ii + 1)]
    owner_x = [owner[0, r] // SIDE for r in range(2)]
    owner_z = [lax.rem(owner[0, r], SIDE) for r in range(2)]
    loads[1].wait()

    def pick(q, _):
        for r in range(2):
            for cc in range(CHUNK):
                for j in range(SIDE):
                    for h in range(2):
                        own[q, j, 2 * r + h, PER * cc : PER * (cc + 1), :] = blk[
                            slot[0, r], q * CHUNK + cc, (2 * j + h) * PER : (2 * j + h + 1) * PER, :
                        ]
        return 0

    lax.fori_loop(0, chunks, pick, 0)
    pl.semaphore_wait(barrier, len(peers))

    def rec_z(k):
        part = pl.ds(me * per_dev, per_dev)
        return send(recg.at[part], recg.at[part], bz_s.at[k - 1], bz_r.at[k - 1], at_z(k))

    def rec_x(k):
        part = pl.ds(x * SIDE * per_dev, SIDE * per_dev)
        return send(recg.at[part], recg.at[part], bx_s.at[k - 1], bx_r.at[k - 1], at_x(k))

    def tmpl_x(q, k):
        return send(
            own.at[q, lax.rem(x + k, SIDE)], rsx.at[q, k - 1], x_s.at[q, k - 1], x_r.at[q, k - 1], at_x(k)
        )

    def tmpl_z(q, k):
        return send(
            cand.at[q, lax.rem(z + k, SIDE)], rsz.at[q, k - 1], z_s.at[q, k - 1], z_r.at[q, k - 1], at_z(k)
        )

    order = (2, 1, 3)

    def start_x(a, b):
        for q in range(a, b):
            for k in order:
                tmpl_x(q, k).start()

    def pass_on(a, b):
        for q in range(a, b):
            for k in order:
                tmpl_x(q, k).wait_recv()
            for i in range(SIDE):
                v = own[q, x, i]
                for k in range(1, SIDE):
                    v = jnp.where(owner_x[i // 2] == lax.rem(x + SIDE - k, SIDE), rsx[q, k - 1, i], v)
                cand[q, i] = v
            for k in order:
                tmpl_z(q, k).start()

    group = 8

    def spread_out(b, _):
        for n in range(group):
            i = b * group + n
            v = recg[i].astype(f32)
            g32[pl.ds(pl.multiple_of(i * channels, 8), channels), :] = v
        return 0

    def weigh(b, band):
        n = group * channels
        a = pl.multiple_of(b * n, 8)
        top, rest = [], []
        for k in range(3):
            v = g32[pl.ds(a + channels * k, n), :]
            sq = v * v
            top.append(sq.astype(bf))
            rest.append((sq - top[k].astype(f32)).astype(bf))
        e = jnp.dot(jnp.concatenate(top, axis=1), band, preferred_element_type=f32)
        e = e + jnp.dot(jnp.concatenate(rest, axis=1), band, preferred_element_type=f32)
        wt32[pl.ds(a, n), :] = 1.0 / jnp.sqrt(jnp.maximum(e, jnp.float32(taps / 4)))
        return band

    def windows(c, _):
        t0 = g32[pl.ds(c, LANES, stride=channels), :].T
        flat = jnp.concatenate([t0] + [pltpu.roll(t0, LANES - k, axis=1) for k in (1, 2)], axis=0)
        turned = jnp.concatenate([pltpu.roll(t0, HALF - k, axis=1) for k in range(3)], axis=0)
        for p in range(2):
            a = 2 * SHIFTS * p
            w = jnp.where(lane < HALF, flat[a : a + used], turned[a + SHIFTS : a + SHIFTS + used])
            right[c, :used, LANES * p : LANES * (p + 1)] = w.astype(bf)
        g = wt32[pl.ds(c, rows, stride=channels), :]
        g = jnp.where(mask[c] != 0, g, 0.0)
        g = jnp.concatenate([g, jnp.zeros((LANES - rows, LANES), f32)], axis=0).T
        for p in range(2):
            a = 2 * SHIFTS * p
            tile[c, p] = jnp.where(
                lane < HALF, g[a : a + SHIFTS], pltpu.roll(g[a + SHIFTS : a + 2 * SHIFTS], HALF, axis=1)
            )
        return 0

    mine = z // 2
    own_z = jnp.where(mine == 0, owner_z[0], owner_z[1])

    def correlate(q, _):
        for k in order:
            tmpl_z(q, k).wait_recv()
        v = cand[q, z]
        for k in range(1, SIDE):
            v = jnp.where(own_z == lax.rem(z + SIDE - k, SIDE), rsz[q, k - 1], v)
        wide = v.astype(f32)
        inv = 1.0 / jnp.sqrt(jnp.sum(wide * wide, axis=1, keepdims=True) + 1e-06)
        unit = (wide * inv).astype(bf).astype(f32)
        for cc in range(CHUNK):
            c = q * CHUNK + cc
            u0 = unit[PER * cc : PER * (cc + 1), :LANES]
            u1 = unit[PER * cc : PER * (cc + 1), LANES:]
            for s in range(0, SHIFTS, 2):
                cols = [[], [], []]
                for b in (s, s + 1):
                    r0 = u0 if b == 0 else pltpu.roll(u0, b, axis=1)
                    r1 = u1 if b == 0 else pltpu.roll(u1, b, axis=1)
                    cols[0].append(jnp.where(lane < b, 0.0, r0))
                    cols[1].append(jnp.where(lane < b, r0, r1))
                    cols[2].append(jnp.where(lane < b, r1, 0.0))
                for p in range(3):
                    lhs[cc, PER * s : PER * (s + 2), LANES * p : LANES * (p + 1)] = jnp.concatenate(
                        cols[p], axis=0
                    ).astype(bf)
            corr = jnp.dot(lhs[cc], right[c], preferred_element_type=f32)
            for p in range(2):
                for s in range(SHIFTS):
                    part = slice(PER * s, PER * (s + 1))
                    acc[p, part, :] += corr[part, LANES * p : LANES * (p + 1)] * tile[c, p, s : s + 1, :]
        return 0

    def correlate_span(a, b):
        lax.fori_loop(a, b, correlate, 0)

    for k in order:
        rec_z(k).start()
    start_x(0, 7)
    pass_on(0, 2)
    for k in order:
        rec_z(k).wait_recv()
    for k in order:
        rec_x(k).start()
    start_x(7, chunks)
    pass_on(2, 7)
    for k in order:
        rec_x(k).wait_recv()
    lax.fori_loop(0, rows // group, spread_out, 0)
    pass_on(7, 8)
    at_p = lax.broadcasted_iota(jnp.int32, (3 * LANES, LANES), 0)
    at_l = lax.broadcasted_iota(jnp.int32, (3 * LANES, LANES), 1)
    band = jnp.where((at_p >= at_l) & (at_p < at_l + taps), 1.0, 0.0).astype(bf)
    lax.fori_loop(0, rows // group, weigh, band)
    pass_on(8, 10)
    lax.fori_loop(0, channels // 2, windows, 0)
    pass_on(10, chunks)
    lax.fori_loop(channels // 2, channels, windows, 0)
    correlate_span(0, chunks)

    count = mask[0]
    for c in range(1, channels):
        count = count + mask[c]
    count_f = jnp.maximum(jnp.full((8, LANES), count, jnp.int32).astype(f32), 1.0)
    gain = (jnp.sqrt(jnp.float32(taps)) / jnp.sqrt(count_f))[:1]
    top = None
    for m in range(PER):
        a, b = (acc[p, pl.ds(m, SHIFTS, stride=PER), :] for p in range(2))
        v = jnp.concatenate([a, pltpu.roll(a, HALF, axis=1), b, pltpu.roll(b, HALF, axis=1)], axis=0)
        v = v.T[:rows] * gain
        nt[pl.ds(m, rows, stride=PER), :] = v
        top = v if m == 0 else jnp.maximum(top, v)
    for t in range(n_tm):
        bl_s[t] = top[per_dev * t : per_dev * (t + 1), :]

    def peak_tm(k):
        return send(bl_s.at[lax.rem(me + k, n_tm)], bl_r.at[k - 1], m_s.at[k - 1], m_r.at[k - 1], at_tm(k))

    place = out.at[mine, pl.ds(pl.multiple_of((2 * x + lax.rem(z, 2)) * PER, PER), PER), :]

    def stack_tm(k):
        return send(sbuf.at[lax.rem(me + k, n_tm)], place, o_s.at[k - 1], o_r.at[k - 1], at_tm(k))

    for k in range(1, n_tm):
        peak_tm(k).start()
    for t in range(n_tm):
        for ii in range(per_dev):
            a = (per_dev * t + ii) * PER
            sbuf[t, :, LANES * ii : LANES * (ii + 1)] = nt[a : a + PER, :].astype(bf)
    for k in range(1, n_tm):
        stack_tm(k).start()
    out[mine, pl.ds(pl.multiple_of((2 * x + lax.rem(z, 2)) * PER, PER), PER), :] = sbuf[me]
    peak = bl_s[me]
    for k in range(1, n_tm):
        peak_tm(k).wait_recv()
        peak = jnp.maximum(peak, bl_r[k - 1])
    near_b[0] = peak

    def peak_near(k):
        return send(near_b.at[0], near_b.at[k], n_s.at[k - 1], n_r.at[k - 1], at_near(k))

    def peak_far(k):
        return send(far_b.at[0], far_b.at[k], f_s.at[k - 1], f_r.at[k - 1], at_far(k))

    for k in range(1, near):
        peak_near(k).start()
    for k in range(1, near):
        peak_near(k).wait_recv()
        peak = jnp.maximum(peak, near_b[k])
    far_b[0] = peak
    for k in range(1, SIDE):
        peak_far(k).start()
    for k in range(1, SIDE):
        peak_far(k).wait_recv()
        peak = jnp.maximum(peak, far_b[k])
    best[...] = peak
    for k in range(1, n_tm):
        stack_tm(k).wait_recv()
    for k in order:
        rec_z(k).wait_send()
        rec_x(k).wait_send()
        for q in range(chunks):
            tmpl_x(q, k).wait_send()
            tmpl_z(q, k).wait_send()
    for k in range(1, n_tm):
        peak_tm(k).wait_send()
        stack_tm(k).wait_send()
    for k in range(1, near):
        peak_near(k).wait_send()
    for k in range(1, SIDE):
        peak_far(k).wait_send()


def on_device(record, templates, owner, slot, mask):
    channels, samples = record.shape
    block, taps = templates.shape[-2:]
    rounds = owner.shape[1]
    n_tm, n_lib = lax.axis_size("tm"), lax.axis_size("lib")
    chunks = channels // CHUNK
    per_dev = samples // LANES
    rows = n_tm * per_dev
    near = n_lib // SIDE
    vm, bf, f32 = pltpu.VMEM, jnp.bfloat16, jnp.float32
    dma = pltpu.SemaphoreType.DMA
    vmem = pl.BlockSpec(memory_space=pltpu.VMEM)
    hbm = pl.BlockSpec(memory_space=pltpu.MemorySpace.HBM)
    piece = (CHUNK * PER, taps)

    stacks, best = pl.pallas_call(
        functools.partial(kernel, n_tm, n_lib),
        out_shape=(
            jax.ShapeDtypeStruct((rounds, block, samples), bf),
            jax.ShapeDtypeStruct((per_dev, LANES), f32),
        ),
        in_specs=[hbm] * 5,
        out_specs=(vmem, vmem),
        scratch_shapes=[
            vm((channels, samples), bf),
            pltpu.SMEM(owner.shape, jnp.int32),
            pltpu.SMEM(slot.shape, jnp.int32),
            pltpu.SMEM(mask.shape, jnp.int32),
            vm(templates.shape[2:], bf),
            vm((chunks, SIDE, SIDE, *piece), bf),
            vm((chunks, SIDE - 1, SIDE, *piece), bf),
            vm((chunks, SIDE, *piece), bf),
            vm((chunks, SIDE - 1, *piece), bf),
            vm((rows, channels, LANES), bf),
            vm((LANES * channels, LANES), f32),
            vm((channels, 3 * LANES, 2 * LANES), bf),
            vm((CHUNK, SHIFTS * PER, 3 * LANES), bf),
            vm((rows * channels, LANES), f32),
            vm((channels, 2, SHIFTS, LANES), f32),
            vm((rows * PER, LANES), f32),
            vm((2, SHIFTS * PER, LANES), f32),
            vm((n_tm, PER, samples), bf),
            vm((n_tm, per_dev, LANES), f32),
            vm((n_tm - 1, per_dev, LANES), f32),
            vm((near, per_dev, LANES), f32),
            vm((SIDE, per_dev, LANES), f32),
            dma((5,)),
            dma((3,)), dma((3,)), dma((3,)), dma((3,)),
            dma((chunks, 3)), dma((chunks, 3)), dma((chunks, 3)), dma((chunks, 3)),
            dma((n_tm - 1,)), dma((n_tm - 1,)), dma((n_tm - 1,)), dma((n_tm - 1,)),
            dma((near - 1,)), dma((near - 1,)), dma((3,)), dma((3,)),
        ],
        compiler_params=pltpu.CompilerParams(
            collective_id=0, has_side_effects=True, vmem_limit_bytes=48 << 20
        ),
        name="match",
    )(*(pltpu.with_memory_space_constraint(a, pltpu.MemorySpace.HBM) for a in (record, templates[0, 0], owner, slot, mask)))
    return stacks[None], best.reshape(samples)


def solution(mesh):
    placed = (
        P(None, "tm"),
        P("lib", "tm", None, None, None, None),
        P("lib", None),
        P("lib", None),
        P(),
    )
    return jax.shard_map(
        on_device,
        mesh=mesh,
        in_specs=placed,
        out_specs=(P("lib", None, None, "tm"), P("tm")),
        check_vma=False,
    )
```

time: 83.6 us -> 68.9 us (0.82)
  Pallas kernels: 76.9 us -> 66.9 us
  local copies, waits for them, and re-layouts: 5.82 us -> 1.24 us
    pallas_call x1, Pallas kernels: 76.9 us -> 66.9 us  [on_device(): pl.pallas_call(functools.partial(kernel, n_tm, n_lib), out_shape=(jax.Sha...]
    unnamed x12 -> x2, local copies, waits for them, and re-layouts: 5.82 us -> 1.24 us
where the time goes in v2:
time: 68.9 us; the launch traced here: 68.8 us
  Pallas kernels  66.9 us (97%)
  local copies, waits for them, and re-layouts  1.24 us (2%)
    pallas_call x1, Pallas kernels, on_device(): pl.pallas_call(functools.partial(kernel, n_tm, n_lib), out_shape=(jax.Sha...  66.9 us

profile of v2, /device:TPU:1, one launch (start us, length us, event | category | flops | bytes accessed | tf_op | source)
XLA Modules:
  0.0 68.8 jit_solution(1998269248883211833)
XLA Ops:
  0.6 66.9 %match.1 = (bf16[2,64,512]{2,1,0:T(8,128)(2,1)S(1)}, f32[4,128]{1,0:T(4,128)S(1)}) custom-call(bf16[24,512]{1,0:T(8,128)(2,1)} %rec_h.1, bf16[4,24,64,256]{3,2,1,0:T(8,128)(2,1)} %bitcast.5, s32[1,2]{1,0:T(1,128)} %owner_h.1, s32[1,2]{1,0:T(1,128)} %slot_h.1, s32[24]{0:T(128)} %mask_h.1), custom_call_target="tpu_custom_call" | custom-call | tf_op jit(solution)/shard_map/match/pallas_call | solution.py:327
  67.5 0.7 copy.9
  68.2 0.6 copy.10

commit v3 on v2

v3 whole, which is shorter than its diff:
```python
import functools

import jax
import jax.numpy as jnp
from jax import lax
from jax.experimental import pallas as pl
from jax.experimental.pallas import tpu as pltpu
from jax.sharding import PartitionSpec as P

MESH = pl.DeviceIdType.MESH
LANES = 128
HALF = LANES // 2
SHIFTS = 32
PER = 8
SIDE = 4
CHUNK = 2
DEPTH = 4


def kernel(
    n_tm, n_lib, rec_h, tmpl, owner_h, slot_h, mask_h, out, best,
    rec, owner, slot, mask, blk, own, rsx, cand, rsz, recg, g32, right, lhs, wt32, tile, nt, acc,
    sbuf, pa_s, pa_r, pb_s, pb_r,
    in_sem, bz_s, bz_r, bx_s, bx_r, x_s, x_r, z_s, z_r, o_s, o_r, m_s, m_r, n_s, n_r, bc_s, bc_r,
):
    slots, channels, block, taps = tmpl.shape
    samples = rec.shape[1]
    me = lax.axis_index("tm")
    lib = lax.axis_index("lib")
    x, z = me // SIDE, lax.rem(me, SIDE)
    near = n_lib // SIDE
    far_at, near_at = lib // near, lax.rem(lib, near)
    chunks = channels // CHUNK
    per_dev = samples // LANES
    rows = n_tm * per_dev
    f32, bf = jnp.float32, jnp.bfloat16

    def at_x(k):
        return {"tm": lax.rem(x + k, SIDE) * SIDE + z}

    def at_z(k):
        return {"tm": x * SIDE + lax.rem(z + k, SIDE)}

    def at_tm(k):
        return {"tm": lax.rem(me + k, n_tm)}

    def at_plane(k):
        kx, ky = k // SIDE, k % SIDE
        return {
            "tm": lax.rem(x + kx, SIDE) * SIDE + z,
            "lib": lax.rem(far_at + ky, SIDE) * near + near_at,
        }

    def column(k):
        return lax.rem(z * near + near_at + k, SIDE * near)

    def at_column(k):
        to = column(k)
        return {"tm": x * SIDE + to // near, "lib": far_at * near + lax.rem(to, near)}

    core = lax.rem(near_at, 2)

    def send(src, dst, s, r, to):
        return pltpu.make_async_remote_copy(
            src_ref=src, dst_ref=dst, send_sem=s, recv_sem=r, device_id=to, device_id_type=MESH
        )

    loads = [
        pltpu.make_async_copy(a, b, in_sem.at[n])
        for n, (a, b) in enumerate(
            ((slot_h, slot), (tmpl, blk), (rec_h, rec), (owner_h, owner), (mask_h, mask))
        )
    ]
    for copy in loads:
        copy.start()
    barrier = pltpu.get_barrier_semaphore()
    peers = [at_column(k) for k in range(1, SIDE * near)] + [at_plane(k) for k in range(1, SIDE * SIDE)]
    for to in peers:
        pl.semaphore_signal(barrier, inc=1, device_id=to, device_id_type=MESH)

    lane = lax.broadcasted_iota(jnp.int32, (1, LANES), 1)
    acc[...] = jnp.zeros_like(acc)
    used = taps + SHIFTS
    right[:, used:, :] = jnp.zeros((channels, right.shape[1] - used, 2 * LANES), bf)
    g32[pl.ds(rows * channels, 2 * channels), :] = jnp.zeros((2 * channels, LANES), f32)
    for n in (0, 2, 3, 4):
        loads[n].wait()
    half = per_dev // 2
    for ii in range(half):
        for at_core in range(2):

            @pl.when(core == at_core)
            def _():
                a = LANES * (at_core * half + ii)
                recg[me, at_core, ii] = rec[:, a : a + LANES]

    owner_x = [owner[0, r] // SIDE for r in range(2)]
    owner_z = [lax.rem(owner[0, r], SIDE) for r in range(2)]
    loads[1].wait()

    def pick(q, _):
        for r in range(2):
            for cc in range(CHUNK):
                for j in range(SIDE):
                    for h in range(2):
                        own[q, j, 2 * r + h, PER * cc : PER * (cc + 1), :] = blk[
                            slot[0, r], q * CHUNK + cc, (2 * j + h) * PER : (2 * j + h + 1) * PER, :
                        ]
        return 0

    lax.fori_loop(0, chunks, pick, 0)
    pl.semaphore_wait(barrier, len(peers))

    def rec_z(k):
        part = recg.at[me, core]
        return send(part, part, bz_s.at[k - 1], bz_r.at[k - 1], at_z(k))

    def rec_x(k):
        part = recg.at[pl.ds(x * SIDE, SIDE), core]
        return send(part, part, bx_s.at[k - 1], bx_r.at[k - 1], at_x(k))

    def rec_core():
        part = recg.at[:, core]
        to = {"lib": lib + 1 - 2 * core}
        return send(part, part, bc_s, bc_r, to)

    def tmpl_x(q, k):
        return send(
            own.at[q, lax.rem(x + k, SIDE)], rsx.at[q, k - 1], x_s.at[q, k - 1], x_r.at[q, k - 1], at_x(k)
        )

    def tmpl_z(q, k):
        return send(
            cand.at[q, lax.rem(z + k, SIDE)], rsz.at[q, k - 1], z_s.at[q, k - 1], z_r.at[q, k - 1], at_z(k)
        )

    order = (2, 1, 3)

    def start_x(a, b):
        for q in range(a, b):
            for k in order:
                tmpl_x(q, k).start()

    def pass_on(a, b):
        for q in range(a, b):
            for k in order:
                tmpl_x(q, k).wait_recv()
            for i in range(SIDE):
                v = own[q, x, i]
                for k in range(1, SIDE):
                    v = jnp.where(owner_x[i // 2] == lax.rem(x + SIDE - k, SIDE), rsx[q, k - 1, i], v)
                cand[q, i] = v
            for k in order:
                tmpl_z(q, k).start()

    group = 8

    def spread_out(b, _):
        for n in range(group):
            i = b * group + n
            v = recg[i // per_dev, lax.rem(i, per_dev) // half, lax.rem(i, half)].astype(f32)
            g32[pl.ds(pl.multiple_of(i * channels, 8), channels), :] = v
        return 0

    def weigh(b, band):
        n = group * channels
        a = pl.multiple_of(b * n, 8)
        top, rest = [], []
        for k in range(3):
            v = g32[pl.ds(a + channels * k, n), :]
            sq = v * v
            top.append(sq.astype(bf))
            rest.append((sq - top[k].astype(f32)).astype(bf))
        e = jnp.dot(jnp.concatenate(top, axis=1), band, preferred_element_type=f32)
        e = e + jnp.dot(jnp.concatenate(rest, axis=1), band, preferred_element_type=f32)
        wt32[pl.ds(a, n), :] = 1.0 / jnp.sqrt(jnp.maximum(e, jnp.float32(taps / 4)))
        return band

    def windows(b, _):
        c = 2 * b
        raw = [g32[pl.ds(c + n, rows, stride=channels), :] for n in range(2)]
        t0 = jnp.concatenate(raw, axis=0).T
        at = lax.rem(lane, HALF)
        flat = [t0] + [jnp.where(at < HALF - k, pltpu.roll(t0, LANES - k, axis=1), 0.0) for k in (1, 2)]
        turned = jnp.concatenate([pltpu.roll(t, HALF, axis=1) for t in flat], axis=0)
        flat = jnp.concatenate(flat, axis=0)
        g = [
            jnp.where(mask[c + n] != 0, wt32[pl.ds(c + n, rows, stride=channels), :], 0.0) for n in range(2)
        ]
        g = jnp.concatenate(g, axis=0).T
        g_turned = pltpu.roll(g, HALF, axis=1)
        for n, (f, t, gf, gt) in enumerate(((flat, turned, g, g_turned), (turned, flat, g_turned, g))):
            for p in range(2):
                a = 2 * SHIFTS * p
                w = jnp.where(lane < HALF, f[a : a + used], t[a + SHIFTS : a + SHIFTS + used])
                right[c + n, :used, LANES * p : LANES * (p + 1)] = w.astype(bf)
                tile[c + n, p] = jnp.where(lane < HALF, gf[a : a + SHIFTS], gt[a + SHIFTS : a + 2 * SHIFTS])
        return 0

    mine = z // 2
    own_z = jnp.where(mine == 0, owner_z[0], owner_z[1])

    def build(q, _):
        for k in order:
            tmpl_z(q, k).wait_recv()
        v = cand[q, z]
        for k in range(1, SIDE):
            v = jnp.where(own_z == lax.rem(z + SIDE - k, SIDE), rsz[q, k - 1], v)
        wide = v.astype(f32)
        inv = 1.0 / jnp.sqrt(jnp.sum(wide * wide, axis=1, keepdims=True) + 1e-06)
        unit = (wide * inv).astype(bf).astype(f32)
        for cc in range(CHUNK):
            c = q * CHUNK + cc
            u0 = unit[PER * cc : PER * (cc + 1), :LANES]
            u1 = unit[PER * cc : PER * (cc + 1), LANES:]
            for s in range(0, SHIFTS, 2):
                cols = [[], [], []]
                for b in (s, s + 1):
                    r0 = u0 if b == 0 else pltpu.roll(u0, b, axis=1)
                    r1 = u1 if b == 0 else pltpu.roll(u1, b, axis=1)
                    cols[0].append(jnp.where(lane < b, 0.0, r0))
                    cols[1].append(jnp.where(lane < b, r0, r1))
                    cols[2].append(jnp.where(lane < b, r1, 0.0))
                for p in range(3):
                    lhs[c, PER * s : PER * (s + 2), LANES * p : LANES * (p + 1)] = jnp.concatenate(
                        cols[p], axis=0
                    ).astype(bf)
        return 0

    def multiply(q, _):
        corr = [jnp.dot(lhs[q * CHUNK + n], right[q * CHUNK + n], preferred_element_type=f32) for n in range(CHUNK)]
        for p in range(2):
            for s in range(SHIFTS):
                part, cols = slice(PER * s, PER * (s + 1)), slice(LANES * p, LANES * (p + 1))
                v = acc[p, part, :]
                for n in range(CHUNK):
                    v = v + corr[n][part, cols] * tile[q * CHUNK + n, p, s : s + 1, :]
                acc[p, part, :] = v
        return 0

    def both(q, _):
        build(q, 0)
        multiply(q, 0)
        return 0

    def step(a, b):
        for q in range(a, b):
            pass_on(q, q + 1)
            if q + DEPTH < chunks:
                start_x(q + DEPTH, q + DEPTH + 1)

    at_p = lax.broadcasted_iota(jnp.int32, (3 * LANES, LANES), 0)
    at_l = lax.broadcasted_iota(jnp.int32, (3 * LANES, LANES), 1)
    band = jnp.where((at_p >= at_l) & (at_p < at_l + taps), 1.0, 0.0).astype(bf)
    pairs, blocks = channels // 2, rows // group

    for k in order:
        rec_z(k).start()
    start_x(0, DEPTH)
    step(0, 4)
    for k in order:
        rec_z(k).wait_recv()
    for k in order:
        rec_x(k).start()
    step(4, 6)
    build(0, 0)
    step(6, 7)
    build(1, 0)
    step(7, 8)
    for k in order:
        rec_x(k).wait_recv()
    rec_core().start()
    step(8, 9)
    rec_core().wait_recv()
    lax.fori_loop(0, blocks, spread_out, 0)
    lax.fori_loop(0, blocks // 2, weigh, band)
    step(9, 10)
    lax.fori_loop(blocks // 2, blocks, weigh, band)
    step(10, 11)
    lax.fori_loop(0, pairs // 2, windows, 0)
    step(11, 12)
    lax.fori_loop(pairs // 2, pairs, windows, 0)
    lax.fori_loop(0, 2, multiply, 0)
    lax.fori_loop(2, chunks, both, 0)

    count = mask[0]
    for c in range(1, channels):
        count = count + mask[c]
    count_f = jnp.maximum(jnp.full((8, LANES), count, jnp.int32).astype(f32), 1.0)
    gain = (jnp.sqrt(jnp.float32(taps)) / jnp.sqrt(count_f))[:1]
    def natural(a, b):
        v = jnp.concatenate([a, pltpu.roll(a, HALF, axis=1), b, pltpu.roll(b, HALF, axis=1)], axis=0)
        return v.T[:rows] * gain

    def template(p, m):
        return acc[p, pl.ds(m, SHIFTS, stride=PER), :]

    top = natural(*(functools.reduce(jnp.maximum, [template(p, m) for m in range(PER)]) for p in range(2)))
    for t in range(SIDE):
        pa_s[t] = top[per_dev * SIDE * t : per_dev * SIDE * (t + 1), :]

    def peak_plane(k):
        return send(pa_s.at[lax.rem(x + k // SIDE, SIDE)], pa_r.at[k - 1], m_s.at[k - 1], m_r.at[k - 1], at_plane(k))

    def peak_column(k):
        return send(pb_s.at[column(k) // near], pb_r.at[k - 1], n_s.at[k - 1], n_r.at[k - 1], at_column(k))

    place = out.at[mine, pl.ds(pl.multiple_of((2 * x + lax.rem(z, 2)) * PER, PER), PER), :]

    def stack_tm(k):
        return send(sbuf.at[lax.rem(me + k, n_tm)], place, o_s.at[k - 1], o_r.at[k - 1], at_tm(k))

    for k in range(1, SIDE * SIDE):
        peak_plane(k).start()
    for m in range(PER):
        nt[pl.ds(m, rows, stride=PER), :] = natural(template(0, m), template(1, m))
    for t in range(n_tm):
        for ii in range(per_dev):
            a = (per_dev * t + ii) * PER
            sbuf[t, :, LANES * ii : LANES * (ii + 1)] = nt[a : a + PER, :].astype(bf)
    for k in range(1, n_tm):
        stack_tm(k).start()
    out[mine, pl.ds(pl.multiple_of((2 * x + lax.rem(z, 2)) * PER, PER), PER), :] = sbuf[me]
    peak = pa_s[x]
    for k in range(1, SIDE * SIDE):
        peak_plane(k).wait_recv()
        peak = jnp.maximum(peak, pa_r[k - 1])
    for t in range(SIDE):
        pb_s[t] = peak[per_dev * t : per_dev * (t + 1), :]
    for k in range(1, SIDE * near):
        peak_column(k).start()
    peak = pb_s[z]
    for k in range(1, SIDE * near):
        peak_column(k).wait_recv()
        peak = jnp.maximum(peak, pb_r[k - 1])
    best[...] = peak
    for k in range(1, n_tm):
        stack_tm(k).wait_recv()
    for k in order:
        rec_z(k).wait_send()
        rec_x(k).wait_send()
        for q in range(chunks):
            tmpl_x(q, k).wait_send()
            tmpl_z(q, k).wait_send()
    rec_core().wait_send()
    for k in range(1, n_tm):
        stack_tm(k).wait_send()
    for k in range(1, SIDE * SIDE):
        peak_plane(k).wait_send()
    for k in range(1, SIDE * near):
        peak_column(k).wait_send()


def on_device(record, templates, owner, slot, mask):
    channels, samples = record.shape
    block, taps = templates.shape[-2:]
    rounds = owner.shape[1]
    n_tm, n_lib = lax.axis_size("tm"), lax.axis_size("lib")
    chunks = channels // CHUNK
    per_dev = samples // LANES
    rows = n_tm * per_dev
    near = n_lib // SIDE
    vm, bf, f32 = pltpu.VMEM, jnp.bfloat16, jnp.float32
    dma = pltpu.SemaphoreType.DMA
    vmem = pl.BlockSpec(memory_space=pltpu.VMEM)
    hbm = pl.BlockSpec(memory_space=pltpu.MemorySpace.HBM)
    piece = (CHUNK * PER, taps)

    stacks, best = pl.pallas_call(
        functools.partial(kernel, n_tm, n_lib),
        out_shape=(
            jax.ShapeDtypeStruct((rounds, block, samples), bf),
            jax.ShapeDtypeStruct((per_dev, LANES), f32),
        ),
        in_specs=[hbm] * 5,
        out_specs=(vmem, vmem),
        scratch_shapes=[
            vm((channels, samples), bf),
            pltpu.SMEM(owner.shape, jnp.int32),
            pltpu.SMEM(slot.shape, jnp.int32),
            pltpu.SMEM(mask.shape, jnp.int32),
            vm(templates.shape[2:], bf),
            vm((chunks, SIDE, SIDE, *piece), bf),
            vm((chunks, SIDE - 1, SIDE, *piece), bf),
            vm((chunks, SIDE, *piece), bf),
            vm((chunks, SIDE - 1, *piece), bf),
            vm((n_tm, 2, per_dev // 2, channels, LANES), bf),
            vm(((rows + 2) * channels, LANES), f32),
            vm((channels, 3 * LANES, 2 * LANES), bf),
            vm((channels, SHIFTS * PER, 3 * LANES), bf),
            vm((rows * channels, LANES), f32),
            vm((channels, 2, SHIFTS, LANES), f32),
            vm((rows * PER, LANES), f32),
            vm((2, SHIFTS * PER, LANES), f32),
            vm((n_tm, PER, samples), bf),
            vm((SIDE, SIDE * per_dev, LANES), f32),
            vm((SIDE * SIDE - 1, SIDE * per_dev, LANES), f32),
            vm((SIDE, per_dev, LANES), f32),
            vm((SIDE * near - 1, per_dev, LANES), f32),
            dma((5,)),
            dma((3,)), dma((3,)), dma((3,)), dma((3,)),
            dma((chunks, 3)), dma((chunks, 3)), dma((chunks, 3)), dma((chunks, 3)),
            dma((n_tm - 1,)), dma((n_tm - 1,)), dma((SIDE * SIDE - 1,)), dma((SIDE * SIDE - 1,)),
            dma((SIDE * near - 1,)), dma((SIDE * near - 1,)), dma, dma,
        ],
        compiler_params=pltpu.CompilerParams(
            collective_id=0, has_side_effects=True, vmem_limit_bytes=48 << 20
        ),
        name="match",
    )(*(pltpu.with_memory_space_constraint(a, pltpu.MemorySpace.HBM) for a in (record, templates[0, 0], owner, slot, mask)))
    return stacks[None], best.reshape(samples)


def solution(mesh):
    placed = (
        P(None, "tm"),
        P("lib", "tm", None, None, None, None),
        P("lib", None),
        P("lib", None),
        P(),
    )
    return jax.shard_map(
        on_device,
        mesh=mesh,
        in_specs=placed,
        out_specs=(P("lib", None, None, "tm"), P("tm")),
        check_vma=False,
    )
```

time: 68.9 us -> 66.6 us (0.967)
  Pallas kernels: 66.9 us -> 64.6 us
    pallas_call x1, Pallas kernels: 66.9 us -> 64.6 us  [on_device(): pl.pallas_call(functools.partial(kernel, n_tm, n_lib), out_shape=(jax.Sha...]
where the time goes in v3:
time: 66.6 us; the launch traced here: 66.4 us
  Pallas kernels  64.6 us (97%)
  local copies, waits for them, and re-layouts  1.24 us (2%)
    pallas_call x1, Pallas kernels, on_device(): pl.pallas_call(functools.partial(kernel, n_tm, n_lib), out_shape=(jax.Sha...  64.6 us

profile of v3, /device:TPU:1, one launch (start us, length us, event | category | flops | bytes accessed | tf_op | source)
XLA Modules:
  0.0 66.4 jit_solution(7963202261963361036)
XLA Ops:
  0.6 64.6 %match.1 = (bf16[2,64,512]{2,1,0:T(8,128)(2,1)S(1)}, f32[4,128]{1,0:T(4,128)S(1)}) custom-call(bf16[24,512]{1,0:T(8,128)(2,1)} %rec_h.1, bf16[4,24,64,256]{3,2,1,0:T(8,128)(2,1)} %bitcast.5, s32[1,2]{1,0:T(1,128)} %owner_h.1, s32[1,2]{1,0:T(1,128)} %slot_h.1, s32[24]{0:T(128)} %mask_h.1), custom_call_target="tpu_custom_call" | custom-call | tf_op jit(solution)/shard_map/match/pallas_call | solution.py:369
  65.2 0.7 copy.9
  65.9 0.6 copy.10

commit v4 on v3

--- a/solution.py
+++ b/solution.py
@@ -21,7 +21,7 @@
     n_tm, n_lib, rec_h, tmpl, owner_h, slot_h, mask_h, out, best,
     rec, owner, slot, mask, blk, own, rsx, cand, rsz, recg, g32, right, lhs, wt32, tile, nt, acc,
     sbuf, pa_s, pa_r, pb_s, pb_r,
-    in_sem, bz_s, bz_r, bx_s, bx_r, x_s, x_r, z_s, z_r, o_s, o_r, m_s, m_r, n_s, n_r, bc_s, bc_r,
+    in_sem, bz_s, bz_r, bx_s, bx_r, x_s, x_r, z_s, z_r, o_s, o_r, m_s, m_r, n_s, n_r, bc_s, bc_r, vouch,
 ):
     slots, channels, block, taps = tmpl.shape
     samples = rec.shape[1]
@@ -51,6 +51,9 @@
             "lib": lax.rem(far_at + ky, SIDE) * near + near_at,
         }
 
+    def at_near(k):
+        return {"lib": far_at * near + lax.rem(near_at + k, near)}
+
     def column(k):
         return lax.rem(z * near + near_at + k, SIDE * near)
 
@@ -74,7 +77,8 @@
     for copy in loads:
         copy.start()
     barrier = pltpu.get_barrier_semaphore()
-    peers = [at_column(k) for k in range(1, SIDE * near)] + [at_plane(k) for k in range(1, SIDE * SIDE)]
+    cousins = [at_near(k) for k in range(1, near)] + [at_plane(k) for k in range(1, SIDE)]
+    peers = [at_z(k) for k in range(1, SIDE)] + [at_x(k) for k in range(1, SIDE)] + cousins
     for to in peers:
         pl.semaphore_signal(barrier, inc=1, device_id=to, device_id_type=MESH)
 
@@ -266,22 +270,28 @@
     build(0, 0)
     step(6, 7)
     build(1, 0)
-    step(7, 8)
+    for to in cousins:
+        pl.semaphore_signal(vouch, inc=1, device_id=to, device_id_type=MESH)
     for k in order:
         rec_x(k).wait_recv()
     rec_core().start()
+    step(7, 8)
+    lax.fori_loop(2, 4, build, 0)
     step(8, 9)
     rec_core().wait_recv()
     lax.fori_loop(0, blocks, spread_out, 0)
+    step(9, 10)
     lax.fori_loop(0, blocks // 2, weigh, band)
-    step(9, 10)
+    step(10, 11)
     lax.fori_loop(blocks // 2, blocks, weigh, band)
-    step(10, 11)
+    step(11, 12)
+    lax.fori_loop(4, 5, build, 0)
     lax.fori_loop(0, pairs // 2, windows, 0)
-    step(11, 12)
+    lax.fori_loop(5, 7, build, 0)
     lax.fori_loop(pairs // 2, pairs, windows, 0)
-    lax.fori_loop(0, 2, multiply, 0)
-    lax.fori_loop(2, chunks, both, 0)
+    lax.fori_loop(7, 9, build, 0)
+    lax.fori_loop(0, 9, multiply, 0)
+    lax.fori_loop(9, chunks, both, 0)
 
     count = mask[0]
     for c in range(1, channels):
@@ -310,6 +320,7 @@
     def stack_tm(k):
         return send(sbuf.at[lax.rem(me + k, n_tm)], place, o_s.at[k - 1], o_r.at[k - 1], at_tm(k))
 
+    pl.semaphore_wait(vouch, len(cousins))
     for k in range(1, SIDE * SIDE):
         peak_plane(k).start()
     for m in range(PER):
@@ -327,7 +338,7 @@
         peak = jnp.maximum(peak, pa_r[k - 1])
     for t in range(SIDE):
         pb_s[t] = peak[per_dev * t : per_dev * (t + 1), :]
-    for k in range(1, SIDE * near):
+    for k in sorted(range(1, SIDE * near), key=lambda k: -min(k, SIDE * near - k)):
         peak_column(k).start()
     peak = pb_s[z]
     for k in range(1, SIDE * near):
@@ -401,7 +412,7 @@
             dma((3,)), dma((3,)), dma((3,)), dma((3,)),
             dma((chunks, 3)), dma((chunks, 3)), dma((chunks, 3)), dma((chunks, 3)),
             dma((n_tm - 1,)), dma((n_tm - 1,)), dma((SIDE * SIDE - 1,)), dma((SIDE * SIDE - 1,)),
-            dma((SIDE * near - 1,)), dma((SIDE * near - 1,)), dma, dma,
+            dma((SIDE * near - 1,)), dma((SIDE * near - 1,)), dma, dma, pltpu.SemaphoreType.REGULAR,
         ],
         compiler_params=pltpu.CompilerParams(
             collective_id=0, has_side_effects=True, vmem_limit_bytes=48 << 20

time: 66.6 us -> 64.6 us (0.970)
  Pallas kernels: 64.6 us -> 62.6 us
    pallas_call x1, Pallas kernels: 64.6 us -> 62.6 us  [on_device(): pl.pallas_call(functools.partial(kernel, n_tm, n_lib), out_shape=(jax.Sha...]
where the time goes in v4:
time: 64.6 us; the launch traced here: 64.5 us
  Pallas kernels  62.6 us (97%)
  local copies, waits for them, and re-layouts  1.24 us (2%)
    pallas_call x1, Pallas kernels, on_device(): pl.pallas_call(functools.partial(kernel, n_tm, n_lib), out_shape=(jax.Sha...  62.6 us

profile of v4, /device:TPU:1, one launch (start us, length us, event | category | flops | bytes accessed | tf_op | source)
XLA Modules:
  0.0 64.5 jit_solution(9334648470243328949)
XLA Ops:
  0.6 62.6 %match.1 = (bf16[2,64,512]{2,1,0:T(8,128)(2,1)S(1)}, f32[4,128]{1,0:T(4,128)S(1)}) custom-call(bf16[24,512]{1,0:T(8,128)(2,1)} %rec_h.1, bf16[4,24,64,256]{3,2,1,0:T(8,128)(2,1)} %bitcast.5, s32[1,2]{1,0:T(1,128)} %owner_h.1, s32[1,2]{1,0:T(1,128)} %slot_h.1, s32[24]{0:T(128)} %mask_h.1), custom_call_target="tpu_custom_call" | custom-call | tf_op jit(solution)/shard_map/match/pallas_call | solution.py:380
  63.2 0.7 %copy.9 = bf16[1,2,64,512]{3,2,1,0:T(8,128)(2,1)} copy(bf16[1,2,64,512]{3,2,1,0:T(8,128)(2,1)S(1)} %bitcast.3) | data formatting | bytes 262144
  63.9 0.6 copy.10

commit v5 on v4

--- a/solution.py
+++ b/solution.py
@@ -14,12 +14,13 @@
 PER = 8
 SIDE = 4
 CHUNK = 2
-DEPTH = 4
+DEPTH = 5
+AHEAD = 6
 
 
 def kernel(
     n_tm, n_lib, rec_h, tmpl, owner_h, slot_h, mask_h, out, best,
-    rec, owner, slot, mask, blk, own, rsx, cand, rsz, recg, g32, right, lhs, wt32, tile, nt, acc,
+    rec, owner, slot, mask, blk, own, rsx, cand, rsz, recg, g32, parts, right, lhs, wt32, tile, nt, acc,
     sbuf, pa_s, pa_r, pb_s, pb_r,
     in_sem, bz_s, bz_r, bx_s, bx_r, x_s, x_r, z_s, z_r, o_s, o_r, m_s, m_r, n_s, n_r, bc_s, bc_r, vouch,
 ):
@@ -87,6 +88,7 @@
     used = taps + SHIFTS
     right[:, used:, :] = jnp.zeros((channels, right.shape[1] - used, 2 * LANES), bf)
     g32[pl.ds(rows * channels, 2 * channels), :] = jnp.zeros((2 * channels, LANES), f32)
+    parts[:, pl.ds(rows, 2)] = jnp.zeros((2, 2, channels, LANES), bf)
     for n in (0, 2, 3, 4):
         loads[n].wait()
     half = per_dev // 2
@@ -163,20 +165,21 @@
         for n in range(group):
             i = b * group + n
             v = recg[i // per_dev, lax.rem(i, per_dev) // half, lax.rem(i, half)].astype(f32)
+            sq = v * v
+            high = sq.astype(bf)
             g32[pl.ds(pl.multiple_of(i * channels, 8), channels), :] = v
+            parts[0, i] = high
+            parts[1, i] = (sq - high.astype(f32)).astype(bf)
         return 0
 
     def weigh(b, band):
         n = group * channels
         a = pl.multiple_of(b * n, 8)
-        top, rest = [], []
-        for k in range(3):
-            v = g32[pl.ds(a + channels * k, n), :]
-            sq = v * v
-            top.append(sq.astype(bf))
-            rest.append((sq - top[k].astype(f32)).astype(bf))
-        e = jnp.dot(jnp.concatenate(top, axis=1), band, preferred_element_type=f32)
-        e = e + jnp.dot(jnp.concatenate(rest, axis=1), band, preferred_element_type=f32)
+        e = None
+        for h in range(2):
+            v = [parts[h, pl.ds(b * group + k, group)].reshape(n, LANES) for k in range(3)]
+            d = jnp.dot(jnp.concatenate(v, axis=1), band, preferred_element_type=f32)
+            e = d if h == 0 else e + d
         wt32[pl.ds(a, n), :] = 1.0 / jnp.sqrt(jnp.maximum(e, jnp.float32(taps / 4)))
         return band
 
@@ -260,38 +263,40 @@
 
     for k in order:
         rec_z(k).start()
-    start_x(0, DEPTH)
-    step(0, 4)
+    start_x(0, AHEAD)
+    pass_on(0, 3)
     for k in order:
         rec_z(k).wait_recv()
     for k in order:
         rec_x(k).start()
-    step(4, 6)
+    start_x(AHEAD, 8)
+    step(3, 6)
     build(0, 0)
-    step(6, 7)
-    build(1, 0)
     for to in cousins:
         pl.semaphore_signal(vouch, inc=1, device_id=to, device_id_type=MESH)
     for k in order:
         rec_x(k).wait_recv()
     rec_core().start()
+    step(6, 7)
+    build(1, 0)
     step(7, 8)
-    lax.fori_loop(2, 4, build, 0)
-    step(8, 9)
     rec_core().wait_recv()
     lax.fori_loop(0, blocks, spread_out, 0)
+    step(8, 9)
+    build(2, 0)
+    lax.fori_loop(0, blocks // 4, weigh, band)
     step(9, 10)
-    lax.fori_loop(0, blocks // 2, weigh, band)
+    build(3, 0)
+    lax.fori_loop(blocks // 4, blocks // 2, weigh, band)
     step(10, 11)
     lax.fori_loop(blocks // 2, blocks, weigh, band)
     step(11, 12)
-    lax.fori_loop(4, 5, build, 0)
     lax.fori_loop(0, pairs // 2, windows, 0)
-    lax.fori_loop(5, 7, build, 0)
+    lax.fori_loop(4, 7, build, 0)
     lax.fori_loop(pairs // 2, pairs, windows, 0)
-    lax.fori_loop(7, 9, build, 0)
-    lax.fori_loop(0, 9, multiply, 0)
-    lax.fori_loop(9, chunks, both, 0)
+    build(7, 0)
+    lax.fori_loop(0, 8, multiply, 0)
+    lax.fori_loop(8, chunks, both, 0)
 
     count = mask[0]
     for c in range(1, channels):
@@ -397,6 +402,7 @@
             vm((chunks, SIDE - 1, *piece), bf),
             vm((n_tm, 2, per_dev // 2, channels, LANES), bf),
             vm(((rows + 2) * channels, LANES), f32),
+            vm((2, rows + 2, channels, LANES), bf),
             vm((channels, 3 * LANES, 2 * LANES), bf),
             vm((channels, SHIFTS * PER, 3 * LANES), bf),
             vm((rows * channels, LANES), f32),

time: 64.6 us -> 64.4 us (level)
  no operation moved by 1% of the time
where the time goes in v5:
time: 64.4 us; the launch traced here: 64.3 us
  Pallas kernels  62.4 us (97%)
  local copies, waits for them, and re-layouts  1.24 us (2%)
    pallas_call x1, Pallas kernels, on_device(): pl.pallas_call(functools.partial(kernel, n_tm, n_lib), out_shape=(jax.Sha...  62.4 us

profile of v5, /device:TPU:1, one launch (start us, length us, event | category | flops | bytes accessed | tf_op | source)
XLA Modules:
  0.0 64.3 jit_solution(8363312627111945281)
XLA Ops:
  0.6 62.4 %match.1 = (bf16[2,64,512]{2,1,0:T(8,128)(2,1)S(1)}, f32[4,128]{1,0:T(4,128)S(1)}) custom-call(bf16[24,512]{1,0:T(8,128)(2,1)} %rec_h.1, bf16[4,24,64,256]{3,2,1,0:T(8,128)(2,1)} %bitcast.5, s32[1,2]{1,0:T(1,128)} %owner_h.1, s32[1,2]{1,0:T(1,128)} %slot_h.1, s32[24]{0:T(128)} %mask_h.1), custom_call_target="tpu_custom_call" | custom-call | tf_op jit(solution)/shard_map/match/pallas_call | solution.py:385
  63.1 0.7 %copy.9 = bf16[1,2,64,512]{3,2,1,0:T(8,128)(2,1)} copy(bf16[1,2,64,512]{3,2,1,0:T(8,128)(2,1)S(1)} %bitcast.3) | data formatting | bytes 262144
  63.7 0.6 copy.10

commit v6 on v5

--- a/solution.py
+++ b/solution.py
@@ -326,7 +326,10 @@
         return send(sbuf.at[lax.rem(me + k, n_tm)], place, o_s.at[k - 1], o_r.at[k - 1], at_tm(k))
 
     pl.semaphore_wait(vouch, len(cousins))
-    for k in range(1, SIDE * SIDE):
+    def hops(k):
+        return sum(min(n, SIDE - n) for n in (k // SIDE, k % SIDE))
+
+    for k in sorted(range(1, SIDE * SIDE), key=lambda k: -hops(k)):
         peak_plane(k).start()
     for m in range(PER):
         nt[pl.ds(m, rows, stride=PER), :] = natural(template(0, m), template(1, m))

time: 64.4 us -> 64.1 us (level)
  no operation moved by 1% of the time
where the time goes in v6:
time: 64.1 us; the launch traced here: 63.9 us
  Pallas kernels  62.1 us (97%)
  local copies, waits for them, and re-layouts  1.24 us (2%)
    pallas_call x1, Pallas kernels, on_device(): pl.pallas_call(functools.partial(kernel, n_tm, n_lib), out_shape=(jax.Sha...  62.1 us

profile of v6, /device:TPU:1, one launch (start us, length us, event | category | flops | bytes accessed | tf_op | source)
XLA Modules:
  0.0 63.9 jit_solution(7227383330996226079)
XLA Ops:
  0.6 62.1 %match.1 = (bf16[2,64,512]{2,1,0:T(8,128)(2,1)S(1)}, f32[4,128]{1,0:T(4,128)S(1)}) custom-call(bf16[24,512]{1,0:T(8,128)(2,1)} %rec_h.1, bf16[4,24,64,256]{3,2,1,0:T(8,128)(2,1)} %bitcast.5, s32[1,2]{1,0:T(1,128)} %owner_h.1, s32[1,2]{1,0:T(1,128)} %slot_h.1, s32[24]{0:T(128)} %mask_h.1), custom_call_target="tpu_custom_call" | custom-call | tf_op jit(solution)/shard_map/match/pallas_call | solution.py:388
  62.7 0.7 %copy.9 = bf16[1,2,64,512]{3,2,1,0:T(8,128)(2,1)} copy(bf16[1,2,64,512]{3,2,1,0:T(8,128)(2,1)S(1)} %bitcast.3) | data formatting | bytes 262144
  63.4 0.6 copy.10
